TPU v7x, 256 devices: a whole 4x4x8 slice. The times are simulated.
256 devices in a mesh: req: 128 (over x, y, z), head: 2 (over core).
Axes of the slice: x: 4, y: 4, z: 8, core: 2. Of those that a mesh axis runs over, the one named last changes fastest.
Arguments:
- verify_x: bfloat16 [128, 5, 2048], P('req'), may hold values from -6 to 6
- prefill_x: bfloat16 [32768, 2048], P('req'), may hold values from -6 to 6
- attn_gain: float32 [2048], replicated, may hold values from 0.25 to 1.75
- w_query: bfloat16 [2048, 2048], P(None, 'head'), may hold values from -0.125 to 0.125
- w_keyval: bfloat16 [2048, 1024], P(None, 'head'), may hold values from -0.125 to 0.125
- qk_gain: float32 [2, 256], replicated, may hold values from 0.25 to 8
- w_out: bfloat16 [2048, 2048], P('head'), may hold values from -0.125 to 0.125
- post_gain: float32 [2048], replicated, may hold values from 0.1 to 1.9
- page_pool: bfloat16 [8192, 16, 1024], P('req', None, 'head'), may hold values from -6 to 6
- outbound: int32 [128, 128], P('req'), may hold values from -1 to 63, as said below
- page_table: int32 [128, 64], P('req'), may hold values from 0 to 191, as said below
- cache_len: int32 [128], P('req'), may hold values from 1 to 1024, as said below
- prompt_len: int32 [128, 4], P('req'), may hold values from 1 to 128, 256 in all within a row
- accepted: int32 [128], P('req'), may hold values from 0 to 5
Outputs:
- verify_out: bfloat16 [128, 5, 2048], P('req', None, 'head')
- prefill_out: bfloat16 [32768, 2048], P('req', 'head')
- verify_kv: bfloat16 [128, 5, 1024], P('req', None, 'head')
- prefill_kv: bfloat16 [32768, 1024], P('req', 'head')
Inputs may be any that keep to these rules, and one draw needn't show every extreme that they name: `outbound`: row s names a page of device s's pool for every device d other than s; the entry at d = s is -1. `page_table`: an entry below 64 names a page of the device's own pool; an entry 64 + s names the page received from device s, s never the device itself. `cache_len`: some request has exactly 1024 cached tokens.
All inputs are finite; a program needn't handle non-finite values.
Results may differ from a plain program's by a relative error of at most 0.015.
The roundings to bfloat16 on the way count: a program that leaves them out, or rounds other values in their place, can miss the bound.
Values may be sent and summed in bfloat16 or wider, within the bound.
No kernel may reach another device: no remote copies, remote signals or barrier semaphores. Data moves between devices by JAX's collectives and lax.ppermute only.
A program may use at most 64 MiB of HBM per device.

v0:
```python
import jax
import jax.numpy as jnp
from jax import lax
from jax.sharding import PartitionSpec as P

HEAD = 256
eps_norm = 1e-06
rope_base = 1000000.0
neg_large = -1e30


def rms_scale(values):
    return values * lax.rsqrt(jnp.mean(values * values, axis=-1, keepdims=True) + eps_norm)


def rotate(values, position):
    half_dim = values.shape[-1] // 2
    inv_freq = rope_base ** (-(jnp.arange(half_dim, dtype=jnp.float32) * 2.0) / values.shape[-1])
    angles = position[:, None, None] * inv_freq[None, None, :]
    cosine = jnp.cos(angles)
    sine_part = jnp.sin(angles)
    first = values[..., :half_dim]
    second = values[..., half_dim:]
    return jnp.concatenate(
        [first * cosine - second * sine_part, second * cosine + first * sine_part], axis=-1
    )


def project(hidden_rows, attn_gain, w_query, w_keyval, qk_gain, position):
    row_count = hidden_rows.shape[0]
    normed = (rms_scale(hidden_rows.astype(jnp.float32)) * attn_gain).astype(jnp.bfloat16)
    query_rows = jnp.dot(normed, w_query, preferred_element_type=jnp.float32).reshape(
        row_count, -1, HEAD
    )
    query_rows = rotate(rms_scale(query_rows) * qk_gain[0], position).astype(jnp.bfloat16)
    keyval = jnp.dot(normed, w_keyval, preferred_element_type=jnp.float32).reshape(
        row_count, -1, 2, HEAD
    )
    key_rows = rotate(rms_scale(keyval[:, :, 0]) * qk_gain[1], position).astype(jnp.bfloat16)
    value_rows = rms_scale(keyval[:, :, 1]).astype(jnp.bfloat16)
    return (query_rows, key_rows, value_rows)


def attend(query_rows, key_rows, value_rows, allowed):
    row_count = query_rows.shape[0]
    groups = key_rows.shape[1]
    grouped = query_rows.reshape(row_count, groups, -1, HEAD)
    scores = jnp.einsum("tgqe,jge->gqtj", grouped, key_rows, preferred_element_type=jnp.float32)
    scores = jnp.where(allowed[None, None], scores, neg_large)
    peak_score = jnp.max(scores, axis=-1, keepdims=True)
    weights = jnp.exp(scores - peak_score)
    denom_sum = jnp.sum(weights, axis=-1, keepdims=True)
    attn_probs = (weights / denom_sum).astype(jnp.bfloat16)
    mixed_heads = jnp.einsum(
        "gqtj,jge->tgqe", attn_probs, value_rows, preferred_element_type=jnp.float32
    )
    return mixed_heads.reshape(row_count, -1).astype(jnp.bfloat16)


def prompt_layout(lengths, row_count):
    prompt_ends = jnp.cumsum(lengths)
    row_index = jnp.arange(row_count, dtype=jnp.int32)
    segment = jnp.sum((row_index[:, None] >= prompt_ends[None, :]).astype(jnp.int32), axis=1)
    starts = prompt_ends - lengths
    which = segment[:, None] == jnp.arange(lengths.shape[0], dtype=jnp.int32)[None, :]
    start_row = jnp.sum(jnp.where(which, starts[None, :], 0), axis=1)
    position = (row_index - start_row).astype(jnp.float32)
    allowed = (segment[:, None] == segment[None, :]) & (row_index[None, :] <= row_index[:, None])
    return (position, allowed)


def on_device(
    verify_x,
    prefill_x,
    attn_gain,
    w_query,
    w_keyval,
    qk_gain,
    w_out,
    post_gain,
    page_pool,
    outbound,
    page_table,
    cache_len,
    prompt_len,
    accepted,
):
    req_count, draft_len, width = verify_x.shape
    pref_rows = prefill_x.shape[0]
    sent_page = outbound[0]
    outgoing = jnp.take(page_pool, jnp.clip(sent_page, 0, page_pool.shape[0] - 1), axis=0)
    outgoing = jnp.where((sent_page >= 0)[:, None, None], outgoing, jnp.zeros_like(outgoing))
    arrived = lax.all_to_all(outgoing, "req", split_axis=0, concat_axis=0, tiled=True)
    pool_now = jnp.concatenate([page_pool, arrived], axis=0)
    verify_pos = (
        (cache_len[:, None] + jnp.arange(draft_len, dtype=jnp.int32)[None, :])
        .astype(jnp.float32)
        .reshape(-1)
    )
    prefill_pos, prefill_allowed = prompt_layout(prompt_len[0], pref_rows)
    all_rows = jnp.concatenate([verify_x.reshape(-1, width), prefill_x], axis=0)
    position = jnp.concatenate([verify_pos, prefill_pos], axis=0)
    query_rows, key_rows, value_rows = project(
        all_rows, attn_gain, w_query, w_keyval, qk_gain, position
    )
    groups = key_rows.shape[1]
    verify_count = req_count * draft_len

    def verify_one(query_part, key_part, value_part, page_list, length):
        cached = jnp.take(pool_now, page_list, axis=0).reshape(-1, groups, 2, HEAD)
        cache_rows = cached.shape[0]
        all_keys = jnp.concatenate([cached[:, :, 0], key_part], axis=0)
        all_values = jnp.concatenate([cached[:, :, 1], value_part], axis=0)
        slot = jnp.arange(cache_rows + draft_len, dtype=jnp.int32)
        step_index = jnp.arange(draft_len, dtype=jnp.int32)
        allowed = jnp.where(
            slot[None, :] < cache_rows,
            slot[None, :] < length,
            slot[None, :] - cache_rows <= step_index[:, None],
        )
        return attend(query_part, all_keys, all_values, allowed)

    verify_attn = jax.vmap(verify_one)(
        query_rows[:verify_count].reshape(req_count, draft_len, -1, HEAD),
        key_rows[:verify_count].reshape(req_count, draft_len, groups, HEAD),
        value_rows[:verify_count].reshape(req_count, draft_len, groups, HEAD),
        page_table,
        cache_len,
    )
    prefill_attn = attend(
        query_rows[verify_count:],
        key_rows[verify_count:],
        value_rows[verify_count:],
        prefill_allowed,
    )
    all_attn = jnp.concatenate([verify_attn.reshape(verify_count, -1), prefill_attn], axis=0)
    partial_rows = jnp.dot(all_attn, w_out, preferred_element_type=jnp.float32)
    half_cols = width // lax.axis_size("head")
    offset = lax.axis_index("head") * half_cols
    summed = lax.psum(partial_rows, "head")
    own_part = lax.dynamic_slice_in_dim(rms_scale(summed), offset, half_cols, 1)
    residual = lax.dynamic_slice_in_dim(all_rows, offset, half_cols, 1).astype(jnp.float32)
    gain_part = lax.dynamic_slice_in_dim(post_gain, offset, half_cols, 0)
    final = (residual + own_part * gain_part).astype(jnp.bfloat16)
    verify_out = final[:verify_count].reshape(req_count, draft_len, half_cols)
    prefill_out = final[verify_count:]
    new_cache = jnp.stack([key_rows, value_rows], axis=2).reshape(all_rows.shape[0], -1)
    verify_cache = new_cache[:verify_count].reshape(req_count, draft_len, -1)
    keep_rows = jnp.arange(draft_len, dtype=jnp.int32)[None, :, None] < accepted[:, None, None]
    verify_kv = jnp.where(keep_rows, verify_cache, jnp.zeros_like(verify_cache))
    prefill_kv = new_cache[verify_count:]
    return (verify_out, prefill_out, verify_kv, prefill_kv)


def solution(mesh):
    placed = (
        P("req", None, None),
        P("req", None),
        P(),
        P(None, "head"),
        P(None, "head"),
        P(),
        P("head", None),
        P(),
        P("req", None, "head"),
        P("req", None),
        P("req", None),
        P("req"),
        P("req", None),
        P("req"),
    )
    return jax.shard_map(
        on_device,
        mesh=mesh,
        in_specs=placed,
        out_specs=(
            P("req", None, "head"),
            P("req", "head"),
            P("req", None, "head"),
            P("req", "head"),
        ),
        check_vma=False,
    )
```

profile of v0, /device:TPU:1, one launch (start us, length us, event | category | flops | bytes accessed | tf_op | source)
XLA Modules:
  0.0 138.2 jit_solution(2135943802772641248)
XLA Ops:
  7.2 0.8 fusion.42
  8.0 0.7 compare_and_fusion
  9.3 3.3 %gather_fusion = bf16[128,16,512]{2,1,0:T(8,128)(2,1)} fusion(bf16[64,16,512]{2,1,0:T(8,128)(2,1)} %param.22, s32[1024]{0:T(1024)S(1)} %pad_clamp_fusion.1), kind=kCustom, calls=%fused_computation | custom fusion | bytes 4194816 | tf_op jit(solution)/shard_map/jit(_take)/gather | solution.py:91
  12.6 3.0 %select_select_fusion = bf16[128,16,512]{2,1,0:T(8,128)(2,1)} fusion(bf16[128,16,512]{2,1,0:T(8,128)(2,1)} %gather_fusion, pred[128]{0:T(512)(128)(4,1)S(1)} %compare_and_fusion, pred[128]{0:T(512)(128)(4,1)S(1)} %compare_bitcast_fusion), kind=kLoop, calls=%fused_computation.11 | loop fusion | flops 2097152 | bytes 4194560 | tf_op jit(solution)/shard_map/jit(_where)/select_n | solution.py:92
  15.6 17.0 %all-to-all-start = ((bf16[128,16,512]{2,1,0:T(8,128)(2,1)}), bf16[128,16,512]{2,1,0:T(8,128)(2,1)}, u32[]{:S(2)}, u32[]{:S(2)}) async-start(bf16[128,16,512]{2,1,0:T(8,128)(2,1)} %select_select_fusion), calls=%async_computation | async-start | bytes 4194304 | tf_op jit(solution)/shard_map/all_to_all | solution.py:93
  34.0 1.6 %fusion.51 = f32[261,512]{1,0:T(8,128)} fusion(bf16[2048,512]{1,0:T(8,128)(2,1)S(1)} %copy-done, f32[2048]{0:T(1024)S(1)} %copy-done.17, f32[261]{0:T(512)S(1)} %add_rsqrt_fusion.4, bf16[256,2048]{1,0:T(8,128)(2,1)S(1)} %copy-done.3, bf16[5,2048]{1,0:T(8,128)(2,1)S(1)} %bitcast.115), kind=kOutput, calls=%fused_computation.125 | convolution fusion | flops 551098368 | bytes 3709972 | tf_op jit(solution)/shard_map/dot_general | solution.py:36
  35.6 2.2 %reshape.682 = f32[261,1,2,256]{3,2,0,1:T(2,128)} reshape(f32[261,512]{1,0:T(8,128)} %fusion.51) | data formatting | bytes 1069056 | tf_op jit(solution)/shard_map/reshape | solution.py:36
  37.8 1.7 %fusion.53 = (f32[261,1,1,256]{3,2,0,1:T(1,128)S(1)}, f32[261,1,1,256]{3,2,0,1:T(1,128)S(1)}) fusion(f32[261,1,2,256]{3,2,0,1:T(2,128)} %reshape.682), kind=kLoop, calls=%fused_computation.126 | loop fusion | bytes 1069056 | tf_op jit(solution)/shard_map/slice | solution.py:40
  39.5 0.7 copy-done.5
  41.3 4.6 %fusion.49 = f32[261,1024]{1,0:T(8,128)} fusion(bf16[2048,1024]{1,0:T(8,128)(2,1)} %param.17, f32[2048]{0:T(1024)S(1)} %copy-done.17, f32[261]{0:T(512)S(1)} %add_rsqrt_fusion.4, bf16[256,2048]{1,0:T(8,128)(2,1)S(1)} %copy-done.3, bf16[5,2048]{1,0:T(8,128)(2,1)S(1)} %bitcast.116), kind=kOutput, calls=%fused_computation.124 | convolution fusion | flops 1098455040 | bytes 6341652 | tf_op jit(solution)/shard_map/dot_general | solution.py:32
  45.9 1.8 %reshape.689 = f32[261,4,256]{2,1,0:T(4,128)S(1)} reshape(f32[261,1024]{1,0:T(8,128)} %fusion.49) | data formatting | bytes 2138112 | tf_op jit(solution)/shard_map/reshape | solution.py:32
  47.7 1.0 multiply_reduce_fusion.1
  48.7 1.0 copy.55
  51.0 0.7 broadcast_in_dim.141
  51.8 1.1 fusion.21
  52.9 1.3 fusion.29
  54.3 1.2 multiply_cosine_fusion
  56.7 1.2 convolution_convert_fusion
  57.9 27.0 %all-to-all-done = bf16[128,16,512]{2,1,0:T(8,128)(2,1)} async-done(((bf16[128,16,512]{2,1,0:T(8,128)(2,1)}), bf16[128,16,512]{2,1,0:T(8,128)(2,1)}, u32[]{:S(2)}, u32[]{:S(2)}) %all-to-all-start) | async-done | bytes 2097184 | tf_op jit(solution)/shard_map/all_to_all | solution.py:93
  84.9 3.5 %pad_maximum_fusion = bf16[192,16,512]{2,1,0:T(8,128)(2,1)} fusion(bf16[128,16,512]{2,1,0:T(8,128)(2,1)} %all-to-all-done, bf16[64,16,512]{2,1,0:T(8,128)(2,1)S(1)} %copy-done.1), kind=kLoop, calls=%fused_computation.2 | loop fusion | flops 1572864 | bytes 6291456 | tf_op jit(solution)/shard_map/concatenate | solution.py:94
  88.4 2.6 %gather_fusion.1 = bf16[64,16,512]{2,1,0:T(8,128)(2,1)S(1)} fusion(bf16[192,16,512]{2,1,0:T(8,128)(2,1)} %pad_maximum_fusion, s32[1024]{0:T(1024)} %pad_clamp_fusion), kind=kCustom, calls=%fused_computation.1 | custom fusion | bytes 2097408 | tf_op jit(solution)/shard_map/vmap(jit(_take))/gather | solution.py:110
  91.1 1.1 gather.12
  92.2 1.5 %copy_select_fusion = bf16[1,1024,1,2,256]{4,1,3,2,0:T(8,128)(2,1)S(1)} fusion(bf16[1,1024,1,2,256]{4,3,1,2,0:T(2,128)(2,1)} %gather.12, pred[1024]{0:T(1024)(128)(4,1)S(1)} %copy-done.15), kind=kLoop, calls=%fused_computation.25 | loop fusion | flops 524288 | bytes 2098176 | tf_op jit(solution)/shard_map/vmap(jit(_take))/select_n | solution.py:110
  94.8 4.9 %fusion.10 = f32[261,2048]{1,0:T(8,128)} fusion(bf16[1024,2048]{1,0:T(8,128)(2,1)} %param.20, bf16[256,1024]{0,1:T(8,128)(2,1)S(1)} %bitcast.123, bf16[5,1024]{0,1:T(8,128)(2,1)S(1)} %copy.59), kind=kOutput, calls=%fused_computation.30 | convolution fusion | flops 1095782400 | bytes 6866944 | tf_op jit(solution)/shard_map/dot_general | solution.py:137
  100.5 1.7 %pad_maximum_fusion.4 = bf16[256,1,2,256]{3,0,2,1:T(8,128)(2,1)} fusion(bf16[261,1,1,256]{3,0,2,1:T(8,128)(2,1)S(1)} %multiply_convert_fusion, bf16[261,1,1,128]{3,0,2,1:T(8,128)(2,1)} %bitcast.111, bf16[261,1,1,128]{3,0,2,1:T(8,128)(2,1)S(1)} %bitcast.109), kind=kLoop, calls=%fused_computation.56 | loop fusion | flops 786432 | bytes 529408 | tf_op jit(solution)/shard_map/stack | solution.py:147
  102.2 1.1 copy.60
  103.3 0.8 copy.61
  104.8 0.7 pad_maximum_fusion.7
  105.5 0.7 broadcast_select_fusion
  106.2 20.9 %all-reduce.2.cloned.1.call-done = f32[261,2048]{1,0:T(8,128)} async-done(((f32[261,2048]{1,0:T(8,128)}), f32[261,2048]{1,0:T(8,128)}) %all-reduce.2.cloned.1.call-update) | async-done | bytes 2138128 | tf_op jit(solution)/shard_map/psum | solution.py:140
  127.1 2.0 %multiply_reduce_fusion = f32[261]{0:T(512)S(1)} fusion(f32[261,2048]{1,0:T(8,128)} %all-reduce.2.cloned.1.call-done), kind=kLoop, calls=%fused_computation.10 | loop fusion | flops 1068795 | bytes 2139156 | tf_op jit(solution)/shard_map/reduce_sum | solution.py:13
  129.8 0.9 slice.103
  (87 shorter events, 8.3 us)
Async XLA Ops:
  7.2 26.8 %copy-start = (bf16[2048,512]{1,0:T(8,128)(2,1)S(1)}, bf16[2048,512]{1,0:T(8,128)(2,1)}, u32[]{:S(2)}) copy-start(bf16[2048,512]{1,0:T(8,128)(2,1)} %param.18) | copy-start | bytes 6291460
  15.6 17.9 %copy-start.18 = (s32[1,64]{1,0:T(1,128)S(1)}, s32[1,64]{1,0:T(1,128)}, u32[]{:S(2)}) copy-start(s32[1,64]{1,0:T(1,128)} %param.24) | copy-start | bytes 772
  15.6 17.9 %copy-start.3 = (bf16[256,2048]{1,0:T(8,128)(2,1)S(1)}, bf16[256,2048]{1,0:T(8,128)(2,1)}, u32[]{:S(2)}) copy-start(bf16[256,2048]{1,0:T(8,128)(2,1)} %param.15) | copy-start | bytes 3145732
  15.6 17.9 %copy-start.12 = (bf16[1,5,2048]{2,1,0:T(8,128)(2,1)S(1)}, bf16[1,5,2048]{2,1,0:T(8,128)(2,1)}, u32[]{:S(2)}) copy-start(bf16[1,5,2048]{2,1,0:T(8,128)(2,1)} %param.14) | copy-start | bytes 61444
  15.6 18.4 %copy-start.17 = (f32[2048]{0:T(1024)S(1)}, f32[2048]{0:T(1024)}, u32[]{:S(2)}) copy-start(f32[2048]{0:T(1024)} %param.16) | copy-start | bytes 24580
  15.6 69.3 %all-to-all-start = ((bf16[128,16,512]{2,1,0:T(8,128)(2,1)}), bf16[128,16,512]{2,1,0:T(8,128)(2,1)}, u32[]{:S(2)}, u32[]{:S(2)}) async-start(bf16[128,16,512]{2,1,0:T(8,128)(2,1)} %select_select_fusion), calls=%async_computation | async-start | bytes 4194304 | tf_op jit(solution)/shard_map/all_to_all | solution.py:93
  32.6 94.4 %all-reduce.2.cloned.1.call-start = ((), (), s32[]{:S(2)}) async-start(), calls=%async_computation.1 | async-start | bytes 4325376 | tf_op jit(solution)/shard_map/psum | solution.py:140
  35.6 4.7 %copy-start.19 = (s32[1,4]{1,0:T(1,128)S(1)}, s32[1,4]{1,0:T(1,128)}, u32[]{:S(2)}) copy-start(s32[1,4]{1,0:T(1,128)} %param.26) | copy-start | bytes 52
  39.4 0.7 copy-start.5
  45.9 5.8 %copy-start.16 = (f32[2,256]{1,0:T(2,128)S(1)}, f32[2,256]{1,0:T(2,128)}, u32[]{:S(2)}) copy-start(f32[2,256]{1,0:T(2,128)} %param.19) | copy-start | bytes 6148
  54.2 1.8 %copy-start.7 = (bf16[261,1,128]{2,0,1:T(8,128)(2,1)}, bf16[261,1,128]{2,0,1:T(8,128)(2,1)S(1)}, u32[]{:S(2)}) copy-start(bf16[261,1,128]{2,0,1:T(8,128)(2,1)S(1)} %get-tuple-element.27) | copy-start | bytes 200452
  56.0 1.9 %copy-start.8 = (bf16[261,4,128]{2,0,1:T(8,128)(2,1)}, bf16[261,4,128]{2,0,1:T(8,128)(2,1)S(1)}, u32[]{:S(2)}) copy-start(bf16[261,4,128]{2,0,1:T(8,128)(2,1)S(1)} %get-tuple-element.20) | copy-start | bytes 801796
  56.0 1.9 %copy-start.10 = (bf16[261,4,128]{2,0,1:T(8,128)(2,1)}, bf16[261,4,128]{2,0,1:T(8,128)(2,1)S(1)}, u32[]{:S(2)}) copy-start(bf16[261,4,128]{2,0,1:T(8,128)(2,1)S(1)} %get-tuple-element.21) | copy-start | bytes 801796
  56.7 1.2 copy-start.13
  56.7 1.2 copy-start.14
  56.7 28.2 %copy-start.1 = (bf16[64,16,512]{2,1,0:T(8,128)(2,1)S(1)}, bf16[64,16,512]{2,1,0:T(8,128)(2,1)}, u32[]{:S(2)}) copy-start(bf16[64,16,512]{2,1,0:T(8,128)(2,1)} %param.22) | copy-start | bytes 3145732
  88.4 3.8 %copy-start.15 = (pred[1024]{0:T(1024)(128)(4,1)S(1)}, pred[1024]{0:T(1024)(128)(4,1)}, u32[]{:S(2)}) copy-start(pred[1024]{0:T(1024)(128)(4,1)} %broadcast_in_dim.141) | copy-start | bytes 3076
  92.2 1.6 %copy-start.9 = (bf16[261,4,128]{2,0,1:T(8,128)(2,1)S(1)}, bf16[261,4,128]{2,0,1:T(8,128)(2,1)}, u32[]{:S(2)}) copy-start(bf16[261,4,128]{2,0,1:T(8,128)(2,1)} %copy-done.8) | copy-start | bytes 801796
  92.2 1.6 %copy-start.11 = (bf16[261,4,128]{2,0,1:T(8,128)(2,1)S(1)}, bf16[261,4,128]{2,0,1:T(8,128)(2,1)}, u32[]{:S(2)}) copy-start(bf16[261,4,128]{2,0,1:T(8,128)(2,1)} %copy-done.10) | copy-start | bytes 801796
  93.8 1.0 copy-start.20
  99.9 0.7 copy-start.6
  99.9 29.2 %copy-start.4 = (bf16[256,2048]{1,0:T(8,128)(2,1)S(1)}, bf16[256,2048]{1,0:T(8,128)(2,1)}, u32[]{:S(2)}) copy-start(bf16[256,2048]{1,0:T(8,128)(2,1)} %param.15) | copy-start | bytes 3145732
  104.8 24.3 %dynamic-slice-start = ((f32[2048]{0:T(1024)}, s32[]{:T(128)}), f32[1024]{0:T(1024)S(1)}, s32[]{:S(2)}) async-start(f32[2048]{0:T(1024)} %param.21, s32[]{:T(128)} %select_n.81), calls=%async_computation.2 | async-start | bytes 8704 | tf_op jit(solution)/shard_map/dynamic_slice | solution.py:143
  127.1 2.3 %copy-start.2 = (f32[261,2048]{1,0:T(8,128)S(1)}, f32[261,2048]{1,0:T(8,128)}, u32[]{:S(2)}) copy-start(f32[261,2048]{1,0:T(8,128)} %all-reduce.2.cloned.1.call-done) | copy-start | bytes 6414340
Sparse Core Ops, SparseCore 0:
  99.9 27.1 all-reduce.1
where the time goes:
time: 139 us; the launch traced here: 138 us
  waiting for transfers between devices  47.9 us (34%)
  other arithmetic  24.3 us (17%)
  local copies, waits for them, and re-layouts  19.8 us (14%)
  starting transfers between devices  17.2 us (12%)
  between operations  15.7 us (11%)
  matrix products  13.3 us (10%)
    all_to_all x1, waiting for transfers between devices, on_device(): lax.all_to_all(outgoing, 'req', split_axis=0, concat_axis=0, tiled=True)  27 us
    psum x1, waiting for transfers between devices, on_device(): summed = lax.psum(partial_rows, 'head')  20.9 us
    all_to_all x1, starting transfers between devices, on_device(): lax.all_to_all(outgoing, 'req', split_axis=0, concat_axis=0, tiled=True)  17 us
    dot_general x1, matrix products, on_device(): partial_rows = jnp.dot(all_attn, w_out, preferred_element_type=jnp.float32)  4.91 us
    reduce_sum x5, other arithmetic, rms_scale(): jnp.mean(values * values, axis=-1, keepdims=True) + eps_norm  4.76 us
    dot_general x1, matrix products, project(): jnp.dot(normed, w_query, preferred_element_type=jnp.float32)  4.6 us
    gather x2, local copies, waits for them, and re-layouts, verify_one(): cached = jnp.take(pool_now, page_list, axis=0).reshape(-1, groups, 2, HEAD)  3.76 us
    concatenate x1, other arithmetic, on_device(): pool_now = jnp.concatenate([page_pool, arrived], axis=0)  3.53 us
  transfers between devices with their start and end apart: 2, of which 2 were waited for; matrix products, arithmetic and copies ran while one was open for 21% of the time, Pallas kernels for 0%

commit v1 on v0

--- a/solution.py
+++ b/solution.py
@@ -137,7 +137,7 @@
     partial_rows = jnp.dot(all_attn, w_out, preferred_element_type=jnp.float32)
     half_cols = width // lax.axis_size("head")
     offset = lax.axis_index("head") * half_cols
-    summed = lax.psum(partial_rows, "head")
+    summed = lax.all_gather(partial_rows, axis_name="head").sum(axis=0)
     own_part = lax.dynamic_slice_in_dim(rms_scale(summed), offset, half_cols, 1)
     residual = lax.dynamic_slice_in_dim(all_rows, offset, half_cols, 1).astype(jnp.float32)
     gain_part = lax.dynamic_slice_in_dim(post_gain, offset, half_cols, 0)

time: 139 us -> 130 us (0.935)
  waiting for transfers between devices: 47.9 us -> 39 us
  other arithmetic: 24.3 us -> 26 us
  local copies, waits for them, and re-layouts: 19.8 us -> 18.3 us
    psum x1 -> x0, waiting for transfers between devices: 20.9 us -> none  [on_device(): summed = lax.psum(partial_rows, 'head')]
    all_gather x0 -> x1, waiting for transfers between devices: none -> 11.8 us  [on_device(): summed = lax.all_gather(partial_rows, axis_name='head').sum(axis=0)]
    reduce_sum x0 -> x1, other arithmetic: none -> 4.2 us  [on_device(): summed = lax.all_gather(partial_rows, axis_name='head').sum(axis=0)]
    another operation x1, other arithmetic: 1.66 us -> 0.07 us  [on_device(): jnp.stack([key_rows, value_rows], axis=2).reshape(all_rows.shape[0], -1)]
  transfers between devices with their start and end apart: 2 -> 2, of which waited for: 2 -> 2; matrix products, arithmetic and copies ran while one was open for 21% -> 19% of each run, Pallas kernels for 0% -> 0%
where the time goes in v1:
time: 130 us
  waiting for transfers between devices  39 us (30%)
  other arithmetic  26 us (20%)
  local copies, waits for them, and re-layouts  18.3 us (14%)
  starting transfers between devices  17.2 us (13%)
  between operations  15.7 us (12%)
  matrix products  13.3 us (10%)
    all_to_all x1, waiting for transfers between devices, on_device(): lax.all_to_all(outgoing, 'req', split_axis=0, concat_axis=0, tiled=True)  27.2 us
    all_to_all x1, starting transfers between devices, on_device(): lax.all_to_all(outgoing, 'req', split_axis=0, concat_axis=0, tiled=True)  17 us
    all_gather x1, waiting for transfers between devices, on_device(): summed = lax.all_gather(partial_rows, axis_name='head').sum(axis=0)  11.8 us
    dot_general x1, matrix products, on_device(): partial_rows = jnp.dot(all_attn, w_out, preferred_element_type=jnp.float32)  4.93 us
    reduce_sum x5, other arithmetic, rms_scale(): jnp.mean(values * values, axis=-1, keepdims=True) + eps_norm  4.76 us
    dot_general x1, matrix products, project(): jnp.dot(normed, w_query, preferred_element_type=jnp.float32)  4.6 us
    reduce_sum x1, other arithmetic, on_device(): summed = lax.all_gather(partial_rows, axis_name='head').sum(axis=0)  4.2 us
    gather x2, local copies, waits for them, and re-layouts, verify_one(): cached = jnp.take(pool_now, page_list, axis=0).reshape(-1, groups, 2, HEAD)  3.76 us
  transfers between devices with their start and end apart: 2, of which 2 were waited for; matrix products, arithmetic and copies ran while one was open for 19% of the time, Pallas kernels for 0%

profile of v1, /device:TPU:1, one launch (start us, length us, event | category | flops | bytes accessed | tf_op | source)
XLA Modules:
  0.0 129.5 jit_solution(15474953056323952004)
XLA Ops:
  7.2 0.8 fusion.41
  8.0 0.7 compare_and_fusion
  8.7 0.7 compare_bitcast_fusion
  9.3 3.3 %gather_fusion = bf16[128,16,512]{2,1,0:T(8,128)(2,1)} fusion(bf16[64,16,512]{2,1,0:T(8,128)(2,1)} %param.22, s32[1024]{0:T(1024)S(1)} %pad_clamp_fusion.1), kind=kCustom, calls=%fused_computation | custom fusion | bytes 4194816 | tf_op jit(solution)/shard_map/jit(_take)/gather | solution.py:91
  12.6 3.0 %select_select_fusion = bf16[128,16,512]{2,1,0:T(8,128)(2,1)} fusion(bf16[128,16,512]{2,1,0:T(8,128)(2,1)} %gather_fusion, pred[128]{0:T(512)(128)(4,1)S(1)} %compare_and_fusion, pred[128]{0:T(512)(128)(4,1)S(1)} %compare_bitcast_fusion), kind=kLoop, calls=%fused_computation.12 | loop fusion | flops 2097152 | bytes 4194560 | tf_op jit(solution)/shard_map/jit(_where)/select_n | solution.py:92
  15.6 17.0 %all-to-all-start = ((bf16[128,16,512]{2,1,0:T(8,128)(2,1)}), bf16[128,16,512]{2,1,0:T(8,128)(2,1)}, u32[]{:S(2)}, u32[]{:S(2)}) async-start(bf16[128,16,512]{2,1,0:T(8,128)(2,1)} %select_select_fusion), calls=%async_computation | async-start | bytes 4194304 | tf_op jit(solution)/shard_map/all_to_all | solution.py:93
  36.2 0.7 broadcast_in_dim.141
  36.9 1.6 %fusion.50 = f32[261,512]{1,0:T(8,128)} fusion(bf16[2048,512]{1,0:T(8,128)(2,1)S(1)} %copy-done, f32[2048]{0:T(1024)S(1)} %copy-done.17, f32[261]{0:T(512)S(1)} %add_rsqrt_fusion.4, bf16[256,2048]{1,0:T(8,128)(2,1)S(1)} %copy-done.3, bf16[5,2048]{1,0:T(8,128)(2,1)S(1)} %bitcast.117), kind=kOutput, calls=%fused_computation.125 | convolution fusion | flops 551098368 | bytes 3709972 | tf_op jit(solution)/shard_map/dot_general | solution.py:36
  38.5 2.2 %reshape.682 = f32[261,1,2,256]{3,2,0,1:T(2,128)} reshape(f32[261,512]{1,0:T(8,128)} %fusion.50) | data formatting | bytes 1069056 | tf_op jit(solution)/shard_map/reshape | solution.py:36
  40.7 1.7 %fusion.52 = (f32[261,1,1,256]{3,2,0,1:T(1,128)S(1)}, f32[261,1,1,256]{3,2,0,1:T(1,128)S(1)}) fusion(f32[261,1,2,256]{3,2,0,1:T(2,128)} %reshape.682), kind=kLoop, calls=%fused_computation.126 | loop fusion | bytes 1069056 | tf_op jit(solution)/shard_map/slice | solution.py:40
  42.3 0.7 copy-done.5
  43.2 4.6 %fusion.48 = f32[261,1024]{1,0:T(8,128)} fusion(bf16[2048,1024]{1,0:T(8,128)(2,1)} %param.17, f32[2048]{0:T(1024)S(1)} %copy-done.17, f32[261]{0:T(512)S(1)} %add_rsqrt_fusion.4, bf16[256,2048]{1,0:T(8,128)(2,1)S(1)} %copy-done.3, bf16[5,2048]{1,0:T(8,128)(2,1)S(1)} %bitcast.118), kind=kOutput, calls=%fused_computation.124 | convolution fusion | flops 1098455040 | bytes 6341652 | tf_op jit(solution)/shard_map/dot_general | solution.py:32
  47.8 1.8 %reshape.689 = f32[261,4,256]{2,1,0:T(4,128)S(1)} reshape(f32[261,1024]{1,0:T(8,128)} %fusion.48) | data formatting | bytes 2138112 | tf_op jit(solution)/shard_map/reshape | solution.py:32
  49.6 1.0 multiply_reduce_fusion.1
  50.6 1.0 copy.55
  51.7 1.1 fusion.20
  52.8 1.2 fusion.28
  54.2 1.1 multiply_cosine_fusion
  56.5 1.2 convolution_convert_fusion
  57.7 27.2 %all-to-all-done = bf16[128,16,512]{2,1,0:T(8,128)(2,1)} async-done(((bf16[128,16,512]{2,1,0:T(8,128)(2,1)}), bf16[128,16,512]{2,1,0:T(8,128)(2,1)}, u32[]{:S(2)}, u32[]{:S(2)}) %all-to-all-start) | async-done | bytes 2097184 | tf_op jit(solution)/shard_map/all_to_all | solution.py:93
  84.9 3.5 %pad_maximum_fusion = bf16[192,16,512]{2,1,0:T(8,128)(2,1)} fusion(bf16[128,16,512]{2,1,0:T(8,128)(2,1)} %all-to-all-done, bf16[64,16,512]{2,1,0:T(8,128)(2,1)S(1)} %copy-done.2), kind=kLoop, calls=%fused_computation.2 | loop fusion | flops 1572864 | bytes 6291456 | tf_op jit(solution)/shard_map/concatenate | solution.py:94
  88.5 2.6 %gather_fusion.1 = bf16[64,16,512]{2,1,0:T(8,128)(2,1)S(1)} fusion(bf16[192,16,512]{2,1,0:T(8,128)(2,1)} %pad_maximum_fusion, s32[1024]{0:T(1024)} %pad_clamp_fusion), kind=kCustom, calls=%fused_computation.1 | custom fusion | bytes 2097408 | tf_op jit(solution)/shard_map/vmap(jit(_take))/gather | solution.py:110
  91.1 1.1 gather.12
  92.2 1.5 %copy_select_fusion = bf16[1,1024,1,2,256]{4,1,3,2,0:T(8,128)(2,1)S(1)} fusion(bf16[1,1024,1,2,256]{4,3,1,2,0:T(2,128)(2,1)} %gather.12, pred[1024]{0:T(1024)(128)(4,1)S(1)} %copy-done.15), kind=kLoop, calls=%fused_computation.26 | loop fusion | flops 524288 | bytes 2098176 | tf_op jit(solution)/shard_map/vmap(jit(_take))/select_n | solution.py:110
  94.8 4.9 %convolution_bitcast_fusion = f32[1,261,2048]{2,1,0:T(8,128)} fusion(bf16[1024,2048]{1,0:T(8,128)(2,1)} %param.20, bf16[256,1024]{0,1:T(8,128)(2,1)S(1)} %bitcast.125, bf16[5,1024]{0,1:T(8,128)(2,1)S(1)} %copy.59), kind=kOutput, calls=%fused_computation.3 | convolution fusion | flops 1095782400 | bytes 6866944 | tf_op jit(solution)/shard_map/dot_general | solution.py:137
  100.9 0.8 copy.61
  101.7 0.7 broadcast_select_fusion
  102.4 11.8 %all-gather.4.cloned.1.call-done = f32[2,261,2048]{2,1,0:T(8,128)} async-done(((f32[1,261,2048]{2,1,0:T(8,128)}), f32[2,261,2048]{2,1,0:T(8,128)}) %all-gather.4.cloned.1.call-update) | async-done | bytes 4276240 | tf_op jit(solution)/shard_map/all_gather | solution.py:140
  114.2 4.2 %reduce_sum.98 = f32[261,2048]{1,0:T(8,128)} reduce(f32[2,261,2048]{2,1,0:T(8,128)} %all-gather.4.cloned.1.call-done, f32[]{:T(128)} %constant.39.clone.1), dimensions={0}, to_apply=%region_11.12 | reduce | flops 534528 | bytes 6414340 | tf_op jit(solution)/shard_map/reduce_sum | solution.py:140
  118.4 2.0 %multiply_reduce_fusion = f32[261]{0:T(512)S(1)} fusion(f32[261,2048]{1,0:T(8,128)} %reduce_sum.98), kind=kLoop, calls=%fused_computation.11 | loop fusion | flops 1068795 | bytes 2139156 | tf_op jit(solution)/shard_map/reduce_sum | solution.py:13
  121.1 0.6 slice_bitcast_fusion.4
  121.7 0.9 slice.103
  (88 shorter events, 6.6 us)
Async XLA Ops:
  7.2 29.7 %copy-start = (bf16[2048,512]{1,0:T(8,128)(2,1)S(1)}, bf16[2048,512]{1,0:T(8,128)(2,1)}, u32[]{:S(2)}) copy-start(bf16[2048,512]{1,0:T(8,128)(2,1)} %param.18) | copy-start | bytes 6291460
  15.6 17.8 %copy-start.18 = (s32[1,64]{1,0:T(1,128)S(1)}, s32[1,64]{1,0:T(1,128)}, u32[]{:S(2)}) copy-start(s32[1,64]{1,0:T(1,128)} %param.24) | copy-start | bytes 772
  15.6 18.5 %copy-start.19 = (s32[1,4]{1,0:T(1,128)S(1)}, s32[1,4]{1,0:T(1,128)}, u32[]{:S(2)}) copy-start(s32[1,4]{1,0:T(1,128)} %param.26) | copy-start | bytes 52
  15.6 18.8 %copy-start.3 = (bf16[256,2048]{1,0:T(8,128)(2,1)S(1)}, bf16[256,2048]{1,0:T(8,128)(2,1)}, u32[]{:S(2)}) copy-start(bf16[256,2048]{1,0:T(8,128)(2,1)} %param.15) | copy-start | bytes 3145732
  15.6 18.8 %copy-start.12 = (bf16[1,5,2048]{2,1,0:T(8,128)(2,1)S(1)}, bf16[1,5,2048]{2,1,0:T(8,128)(2,1)}, u32[]{:S(2)}) copy-start(bf16[1,5,2048]{2,1,0:T(8,128)(2,1)} %param.14) | copy-start | bytes 61444
  15.6 21.3 %copy-start.17 = (f32[2048]{0:T(1024)S(1)}, f32[2048]{0:T(1024)}, u32[]{:S(2)}) copy-start(f32[2048]{0:T(1024)} %param.16) | copy-start | bytes 24580
  15.6 69.3 %all-to-all-start = ((bf16[128,16,512]{2,1,0:T(8,128)(2,1)}), bf16[128,16,512]{2,1,0:T(8,128)(2,1)}, u32[]{:S(2)}, u32[]{:S(2)}) async-start(bf16[128,16,512]{2,1,0:T(8,128)(2,1)} %select_select_fusion), calls=%async_computation | async-start | bytes 4194304 | tf_op jit(solution)/shard_map/all_to_all | solution.py:93
  32.6 81.6 %all-gather.4.cloned.1.call-start = ((), (), s32[]{:S(2)}) async-start(), calls=%async_computation.1 | async-start | bytes 6488064 | tf_op jit(solution)/shard_map/all_gather | solution.py:140
  42.3 0.7 copy-start.5
  47.8 3.9 %copy-start.16 = (f32[2,256]{1,0:T(2,128)S(1)}, f32[2,256]{1,0:T(2,128)}, u32[]{:S(2)}) copy-start(f32[2,256]{1,0:T(2,128)} %param.19) | copy-start | bytes 6148
  54.0 1.7 %copy-start.6 = (bf16[261,1,128]{2,0,1:T(8,128)(2,1)}, bf16[261,1,128]{2,0,1:T(8,128)(2,1)S(1)}, u32[]{:S(2)}) copy-start(bf16[261,1,128]{2,0,1:T(8,128)(2,1)S(1)} %get-tuple-element.27) | copy-start | bytes 200452
  55.7 1.9 %copy-start.8 = (bf16[261,4,128]{2,0,1:T(8,128)(2,1)}, bf16[261,4,128]{2,0,1:T(8,128)(2,1)S(1)}, u32[]{:S(2)}) copy-start(bf16[261,4,128]{2,0,1:T(8,128)(2,1)S(1)} %get-tuple-element.20) | copy-start | bytes 801796
  55.7 1.9 %copy-start.10 = (bf16[261,4,128]{2,0,1:T(8,128)(2,1)}, bf16[261,4,128]{2,0,1:T(8,128)(2,1)S(1)}, u32[]{:S(2)}) copy-start(bf16[261,4,128]{2,0,1:T(8,128)(2,1)S(1)} %get-tuple-element.21) | copy-start | bytes 801796
  56.4 1.2 copy-start.13
  56.4 1.2 copy-start.14
  56.4 28.5 %copy-start.2 = (bf16[64,16,512]{2,1,0:T(8,128)(2,1)S(1)}, bf16[64,16,512]{2,1,0:T(8,128)(2,1)}, u32[]{:S(2)}) copy-start(bf16[64,16,512]{2,1,0:T(8,128)(2,1)} %param.22) | copy-start | bytes 3145732
  88.5 3.8 %copy-start.15 = (pred[1024]{0:T(1024)(128)(4,1)S(1)}, pred[1024]{0:T(1024)(128)(4,1)}, u32[]{:S(2)}) copy-start(pred[1024]{0:T(1024)(128)(4,1)} %broadcast_in_dim.141) | copy-start | bytes 3076
  92.2 1.6 %copy-start.9 = (bf16[261,4,128]{2,0,1:T(8,128)(2,1)S(1)}, bf16[261,4,128]{2,0,1:T(8,128)(2,1)}, u32[]{:S(2)}) copy-start(bf16[261,4,128]{2,0,1:T(8,128)(2,1)} %copy-done.8) | copy-start | bytes 801796
  92.2 1.6 %copy-start.11 = (bf16[261,4,128]{2,0,1:T(8,128)(2,1)S(1)}, bf16[261,4,128]{2,0,1:T(8,128)(2,1)}, u32[]{:S(2)}) copy-start(bf16[261,4,128]{2,0,1:T(8,128)(2,1)} %copy-done.10) | copy-start | bytes 801796
  93.8 1.0 copy-start.20
  99.8 0.9 copy-start.7
  114.2 6.2 %copy-start.4 = (bf16[256,2048]{1,0:T(8,128)(2,1)S(1)}, bf16[256,2048]{1,0:T(8,128)(2,1)}, u32[]{:S(2)}) copy-start(bf16[256,2048]{1,0:T(8,128)(2,1)} %param.15) | copy-start | bytes 3145732
  118.4 2.3 %copy-start.1 = (f32[261,2048]{1,0:T(8,128)S(1)}, f32[261,2048]{1,0:T(8,128)}, u32[]{:S(2)}) copy-start(f32[261,2048]{1,0:T(8,128)} %reduce_sum.98) | copy-start | bytes 6414340
  118.4 2.3 %dynamic-slice-start = ((f32[2048]{0:T(1024)}, s32[]{:T(128)}), f32[1024]{0:T(1024)S(1)}, s32[]{:S(2)}) async-start(f32[2048]{0:T(1024)} %param.21, s32[]{:T(128)} %select_n.81), calls=%async_computation.2 | async-start | bytes 8704 | tf_op jit(solution)/shard_map/dynamic_slice | solution.py:143
Sparse Core Ops, SparseCore 0:
  99.9 14.2 all-gather.3
